TPU v7x, 256 devices: a whole 4x4x8 slice. The times are simulated.
256 devices in a mesh: dp: 8 (over x, core), context: 32 (over z, y).
Axes of the slice: x: 4, y: 4, z: 8, core: 2. Of those that a mesh axis runs over, the one named last changes fastest.
Arguments:
- inputs: bfloat16 [8, 16384, 1024], P('dp', 'context'), may hold values from -6 to 6
- step_size: float32 [8, 16384], P('dp', 'context'), may hold values from 0.25 to 16387
- decay_rate: float32 [256], replicated, may hold values from 1.2207031e-05 to 0.125
- frequency: float32 [256], replicated, may hold values from -0.5 to 0.5
- input_proj: bfloat16 [1024, 512], replicated, may hold values from -0.1875 to 0.1875
- output_proj: bfloat16 [1024, 512], replicated, may hold values from -0.25 to 0.25
- skip_gain: float32 [1024], replicated, may hold values from 0.25 to 1.75
- cotangent: bfloat16 [8, 16384, 1024], P('dp', 'context'), may hold values from -6 to 6
Outputs:
- outputs: bfloat16 [8, 16384, 1024], P('dp', 'context')
- input_grad: bfloat16 [8, 16384, 1024], P('dp', 'context')
- input_proj_grad: float32 [1024, 512], P('context')
- output_proj_grad: float32 [1024, 512], P('context')
All inputs are finite; a program needn't handle non-finite values.
Results may differ from a plain program's by a relative error of at most 0.0036.
Values sent between devices are 32-bit elements; how exact they have to be, the bound alone decides.
A program may use at most 64 MiB of HBM per device.

v0:
```python
import jax
import jax.numpy as jnp
from jax import lax
from jax.sharding import PartitionSpec as P


def prefix(x, axis, combine, identity, reverse):
    peers, place = (lax.axis_size(axis), lax.axis_index(axis))
    everything = jax.tree.map(lambda part: lax.all_gather(part, axis), x)
    start = jax.tree.map(
        lambda part, zero: jnp.broadcast_to(jnp.asarray(zero, part.dtype), part.shape), x, identity
    )

    def lap(k, before):
        at = peers - 1 - k if reverse else k
        reached = at > place if reverse else at < place
        new = combine(before, jax.tree.map(lambda part: part[at], everything))
        return jax.tree.map(lambda a, b: jnp.where(reached, a, b), new, before)

    return lax.fori_loop(0, peers, lap, start)


def complex_combine(earlier_pair, later_pair):
    early_are, early_aim, early_bre, early_bim = earlier_pair
    later_are, later_aim, later_bre, later_bim = later_pair
    return (
        later_are * early_are - later_aim * early_aim,
        later_are * early_aim + later_aim * early_are,
        later_are * early_bre - later_aim * early_bim + later_bre,
        later_are * early_bim + later_aim * early_bre + later_bim,
    )


def on_device(
    inputs, step_size, decay_rate, frequency, input_proj, output_proj, skip_gain, cotangent
):
    batch_count, row_count, model_width = inputs.shape
    state_count = decay_rate.shape[0]
    damping = jnp.exp(-step_size[:, :, None] * decay_rate)
    phase_turn = step_size[:, :, None] * frequency
    lam_re = damping * jnp.cos(phase_turn)
    lam_im = damping * jnp.sin(phase_turn)
    norm_gain = jnp.sqrt(-jnp.expm1(-2.0 * decay_rate))
    pair_gain = jnp.concatenate([norm_gain, norm_gain])
    flat_in = inputs.reshape(batch_count * row_count, model_width)
    flat_cot = cotangent.reshape(batch_count * row_count, model_width)
    drive_term = (
        jnp.dot(flat_in, input_proj, preferred_element_type=jnp.float32).reshape(
            batch_count, row_count, 2 * state_count
        )
        * pair_gain
    )
    local_fwd = lax.associative_scan(
        complex_combine,
        (lam_re, lam_im, drive_term[..., :state_count], drive_term[..., state_count:]),
        axis=1,
    )
    fwd_summary = (
        local_fwd[0][:, -1],
        local_fwd[1][:, -1],
        local_fwd[2][:, -1],
        local_fwd[3][:, -1],
    )
    adjoint_drive = jnp.dot(flat_cot, output_proj, preferred_element_type=jnp.float32).reshape(
        batch_count, row_count, 2 * state_count
    )
    next_re = jnp.concatenate([lam_re[:, 1:], jnp.ones_like(lam_re[:, :1])], axis=1)
    next_im = jnp.concatenate([-lam_im[:, 1:], jnp.zeros_like(lam_im[:, :1])], axis=1)
    local_back = lax.associative_scan(
        complex_combine,
        (next_re, next_im, adjoint_drive[..., :state_count], adjoint_drive[..., state_count:]),
        axis=1,
        reverse=True,
    )
    first_re = lam_re[:, 0]
    first_im = -lam_im[:, 0]
    back_summary = (
        first_re * local_back[0][:, 0] - first_im * local_back[1][:, 0],
        first_re * local_back[1][:, 0] + first_im * local_back[0][:, 0],
        first_re * local_back[2][:, 0] - first_im * local_back[3][:, 0],
        first_re * local_back[3][:, 0] + first_im * local_back[2][:, 0],
    )
    unit_pair = (
        jnp.ones_like(fwd_summary[0]),
        jnp.zeros_like(fwd_summary[0]),
        jnp.zeros_like(fwd_summary[0]),
        jnp.zeros_like(fwd_summary[0]),
    )
    fwd_carry = prefix(fwd_summary, "context", complex_combine, unit_pair, False)
    back_carry = prefix(back_summary, "context", complex_combine, unit_pair, True)
    carry_re, carry_im = (fwd_carry[2], fwd_carry[3])
    inflow_re, inflow_im = (back_carry[2], back_carry[3])
    state_re = local_fwd[2] + local_fwd[0] * carry_re[:, None] - local_fwd[1] * carry_im[:, None]
    state_im = local_fwd[3] + local_fwd[0] * carry_im[:, None] + local_fwd[1] * carry_re[:, None]
    back_re = (
        local_back[2] + local_back[0] * inflow_re[:, None] - local_back[1] * inflow_im[:, None]
    )
    back_im = (
        local_back[3] + local_back[0] * inflow_im[:, None] + local_back[1] * inflow_re[:, None]
    )
    last_contract = (((1,), (1,)), ((), ()))
    state_pairs = (
        jnp.concatenate([state_re, state_im], axis=-1)
        .astype(jnp.bfloat16)
        .reshape(batch_count * row_count, 2 * state_count)
    )
    mixed = lax.dot_general(
        state_pairs, output_proj, last_contract, preferred_element_type=jnp.float32
    ).reshape(batch_count, row_count, model_width)
    outputs = (mixed + skip_gain * inputs.astype(jnp.float32)).astype(jnp.bfloat16)
    adjoint_pairs = (
        (jnp.concatenate([back_re, back_im], axis=-1) * pair_gain)
        .astype(jnp.bfloat16)
        .reshape(batch_count * row_count, 2 * state_count)
    )
    back_in = lax.dot_general(
        adjoint_pairs, input_proj, last_contract, preferred_element_type=jnp.float32
    ).reshape(batch_count, row_count, model_width)
    input_grad = (back_in + skip_gain * cotangent.astype(jnp.float32)).astype(jnp.bfloat16)
    context_count = lax.axis_size("context")
    grad_scale = float(batch_count * row_count * lax.axis_size("dp") * context_count) ** (-0.5)
    token_contract = (((0,), (0,)), ((), ()))
    grad_in_part = lax.dot_general(
        flat_in, adjoint_pairs, token_contract, preferred_element_type=jnp.float32
    )
    grad_out_part = lax.dot_general(
        flat_cot, state_pairs, token_contract, preferred_element_type=jnp.float32
    )
    shares = lax.psum_scatter(
        jnp.concatenate([grad_in_part, grad_out_part], axis=1) * grad_scale,
        "context",
        scatter_dimension=0,
        tiled=True,
    )
    my_rows = lax.psum(shares, "dp")
    return (outputs, input_grad, my_rows[:, : 2 * state_count], my_rows[:, 2 * state_count :])


def solution(mesh):
    in_specs = (
        P("dp", "context", None),
        P("dp", "context"),
        P(),
        P(),
        P(),
        P(),
        P(),
        P("dp", "context", None),
    )
    out_specs = (
        P("dp", "context", None),
        P("dp", "context", None),
        P("context", None),
        P("context", None),
    )
    return jax.shard_map(
        on_device, mesh=mesh, in_specs=in_specs, out_specs=out_specs, check_vma=False
    )
```

profile of v0, /device:TPU:8, one launch (start us, length us, event | category | flops | bytes accessed | tf_op | source)
XLA Modules:
  0.0 1172.5 jit_solution(17357458822823251579)
XLA Ops:
  8.0 2.7 fusion.12
  29.8 2.9 slice.1317
  32.8 2.9 slice.1323
  37.0 3.0 slice.1333
  40.0 3.0 slice.1320
  43.0 3.0 slice.1326
  46.0 3.0 slice.1328
  223.5 3.0 slice.1453
  226.6 3.0 slice.1458
  229.6 3.0 slice.1496
  253.1 2.6 pad.548
  443.0 4.7 rev.19
  447.8 45.9 %all_gather.32 = f32[32,1,256]{2,1,0:T(1,128)S(1)} all-gather(f32[1,1,256]{2,1,0:T(1,128)} %get-tuple-element.448), channel_id=1, replica_groups=mesh['dp'=8,'context'=32] {'context'}, dimensions={0}, use_global_device_ids=true | all-gather | bytes 33792 | tf_op jit(solution)/shard_map/all_gather | solution.py:9
  493.7 40.8 %all_gather.33 = f32[32,1,256]{2,1,0:T(1,128)S(1)} all-gather(f32[1,1,256]{2,1,0:T(1,128)} %get-tuple-element.447), channel_id=1, replica_groups=mesh['dp'=8,'context'=32] {'context'}, dimensions={0}, use_global_device_ids=true | all-gather | bytes 33792 | tf_op jit(solution)/shard_map/all_gather | solution.py:9
  534.5 41.9 %all_gather.34 = f32[32,1,256]{2,1,0:T(1,128)S(1)} all-gather(f32[1,1,256]{2,1,0:T(1,128)} %get-tuple-element.446), channel_id=1, replica_groups=mesh['dp'=8,'context'=32] {'context'}, dimensions={0}, use_global_device_ids=true | all-gather | bytes 33792 | tf_op jit(solution)/shard_map/all_gather | solution.py:9
  576.4 40.8 %all_gather.35 = f32[32,1,256]{2,1,0:T(1,128)S(1)} all-gather(f32[1,1,256]{2,1,0:T(1,128)} %get-tuple-element.445), channel_id=1, replica_groups=mesh['dp'=8,'context'=32] {'context'}, dimensions={0}, use_global_device_ids=true | all-gather | bytes 33792 | tf_op jit(solution)/shard_map/all_gather | solution.py:9
  617.2 37.7 %while.35 = (s32[]{:T(128)}, f32[1,256]{1,0:T(1,128)}, f32[1,256]{1,0:T(1,128)}, s32[]{:T(128)}, f32[32,1,256]{2,1,0:T(1,128)S(1)}, /*index=5*/f32[32,1,256]{2,1...) while((s32[]{:T(128)}, f32[1,256]{1,0:T(1,128)}, ...), condition=%wide.region_3.4_spmd.clone, body=%wide.region_2.3_spmd.clone.sunk | while | flops 3080 | bytes 8379 | solution.py:20
  654.9 2.6 rev.17
  657.5 2.6 rev.16
  677.2 41.9 %all_gather.31 = f32[32,1,256]{2,1,0:T(1,128)S(1)} all-gather(f32[1,1,256]{2,1,0:T(1,128)S(1)} %slice_add_fusion.64), channel_id=1, replica_groups=mesh['dp'=8,'context'=32] {'context'}, dimensions={0}, use_global_device_ids=true | all-gather | bytes 33792 | tf_op jit(solution)/shard_map/all_gather | solution.py:9
  721.3 40.7 %all_gather.29 = f32[32,1,256]{2,1,0:T(1,128)S(1)} all-gather(f32[1,1,256]{2,1,0:T(1,128)S(1)} %slice_add_fusion.66), channel_id=1, replica_groups=mesh['dp'=8,'context'=32] {'context'}, dimensions={0}, use_global_device_ids=true | all-gather | bytes 33792 | tf_op jit(solution)/shard_map/all_gather | solution.py:9
  763.6 2.6 pad.510
  766.3 2.7 pad.511
  769.7 41.9 %all_gather.28 = f32[32,1,256]{2,1,0:T(1,128)S(1)} all-gather(f32[1,1,256]{2,1,0:T(1,128)S(1)} %slice_add_fusion.67), channel_id=1, replica_groups=mesh['dp'=8,'context'=32] {'context'}, dimensions={0}, use_global_device_ids=true | all-gather | bytes 33792 | tf_op jit(solution)/shard_map/all_gather | solution.py:9
  811.6 2.6 pad.477
  818.2 40.7 %all_gather.30 = f32[32,1,256]{2,1,0:T(1,128)S(1)} all-gather(f32[1,1,256]{2,1,0:T(1,128)S(1)} %slice_add_fusion.65), channel_id=1, replica_groups=mesh['dp'=8,'context'=32] {'context'}, dimensions={0}, use_global_device_ids=true | all-gather | bytes 33792 | tf_op jit(solution)/shard_map/all_gather | solution.py:9
  865.9 2.6 maximum_multiply_fusion
  868.6 5.4 copy.16
  875.1 2.9 fusion.4
  878.1 217.4 %reduce-scatter.4.cloned.1.call-done = f32[32,1024]{1,0:T(8,128)} async-done(((f32[1024,1024]{1,0:T(8,128)}), f32[32,1024]{1,0:T(8,128)}) %reduce-scatter.4.cloned.1.call-update) | async-done | bytes 131088
  1097.5 3.3 fusion.5
  1100.7 62.4 %all-reduce.150.cloned.1.call-done = f32[32,1024]{0,1:T(8,128)} async-done(((f32[32,1024]{0,1:T(8,128)}), f32[32,1024]{0,1:T(8,128)}) %all-reduce.150.cloned.1.call-update) | async-done | bytes 131088 | tf_op jit(solution)/shard_map/psum | solution.py:135
  (908 shorter events, 477.5 us)
Async XLA Ops:
  7.2 272.5 %copy-start = (bf16[1024,512]{1,0:T(8,128)(2,1)S(1)}, bf16[1024,512]{1,0:T(8,128)(2,1)}, u32[]{:S(2)}) copy-start(bf16[1024,512]{1,0:T(8,128)(2,1)} %param.16) | copy-start | bytes 3145732
  7.2 1088.3 %reduce-scatter.4.cloned.1.call-start = ((), (), s32[]{:S(2)}) async-start(), calls=%async_computation.2 | async-start | bytes 4325376
  65.9 103.9 %copy-start.35 = (f32[1,128,256]{2,1,0:T(8,128)}, f32[1,128,256]{2,1,0:T(8,128)S(1)}, u32[]{:S(2)}) copy-start(f32[1,128,256]{2,1,0:T(8,128)S(1)} %get-tuple-element.512) | copy-start | bytes 393220
  290.7 125.0 %copy-start.19 = (f32[1,256,256]{2,1,0:T(8,128)}, f32[1,256,256]{2,1,0:T(8,128)S(1)}, u32[]{:S(2)}) copy-start(f32[1,256,256]{2,1,0:T(8,128)S(1)} %get-tuple-element.471) | copy-start | bytes 786436
  304.0 104.0 %copy-start.36 = (f32[1,128,256]{2,1,0:T(8,128)}, f32[1,128,256]{2,1,0:T(8,128)S(1)}, u32[]{:S(2)}) copy-start(f32[1,128,256]{2,1,0:T(8,128)S(1)} %get-tuple-element.520) | copy-start | bytes 393220
  423.9 233.6 %copy-start.12 = (f32[1,512,256]{2,1,0:T(8,128)S(1)}, f32[1,512,256]{2,1,0:T(8,128)}, u32[]{:S(2)}) copy-start(f32[1,512,256]{2,1,0:T(8,128)} %add.1249) | copy-start | bytes 1572868
  425.4 229.5 %copy-start.13 = (f32[1,512,256]{2,1,0:T(8,128)S(1)}, f32[1,512,256]{2,1,0:T(8,128)}, u32[]{:S(2)}) copy-start(f32[1,512,256]{2,1,0:T(8,128)} %add.1274) | copy-start | bytes 1572868
  426.8 233.4 %copy-start.14 = (f32[1,512,256]{2,1,0:T(8,128)S(1)}, f32[1,512,256]{2,1,0:T(8,128)}, u32[]{:S(2)}) copy-start(f32[1,512,256]{2,1,0:T(8,128)} %add.1276) | copy-start | bytes 1572868
  442.9 219.8 %copy-start.128 = (f32[1,1,256]{2,1,0:T(1,128)S(1)}, f32[1,1,256]{2,1,0:T(1,128)}, u32[]{:S(2)}) copy-start(f32[1,1,256]{2,1,0:T(1,128)} %get-tuple-element.607) | copy-start | bytes 3076
  442.9 219.8 %copy-start.129 = (f32[1,1,256]{2,1,0:T(1,128)S(1)}, f32[1,1,256]{2,1,0:T(1,128)}, u32[]{:S(2)}) copy-start(f32[1,1,256]{2,1,0:T(1,128)} %get-tuple-element.608) | copy-start | bytes 3076
  442.9 219.8 %copy-start.130 = (f32[1,1,256]{2,1,0:T(1,128)S(1)}, f32[1,1,256]{2,1,0:T(1,128)}, u32[]{:S(2)}) copy-start(f32[1,1,256]{2,1,0:T(1,128)} %get-tuple-element.627) | copy-start | bytes 3076
  442.9 219.8 %copy-start.131 = (f32[1,1,256]{2,1,0:T(1,128)S(1)}, f32[1,1,256]{2,1,0:T(1,128)}, u32[]{:S(2)}) copy-start(f32[1,1,256]{2,1,0:T(1,128)} %get-tuple-element.638) | copy-start | bytes 3076
  443.0 219.9 %copy-start.90 = (f32[1,2,256]{2,1,0:T(2,128)S(1)}, f32[1,2,256]{2,1,0:T(2,128)}, u32[]{:S(2)}) copy-start(f32[1,2,256]{2,1,0:T(2,128)} %get-tuple-element.648) | copy-start | bytes 6148
  443.0 219.9 %copy-start.89 = (f32[1,2,256]{2,1,0:T(2,128)S(1)}, f32[1,2,256]{2,1,0:T(2,128)}, u32[]{:S(2)}) copy-start(f32[1,2,256]{2,1,0:T(2,128)} %get-tuple-element.647) | copy-start | bytes 6148
  447.7 215.2 %copy-start.126 = (f32[1,1,256]{2,1,0:T(1,128)S(1)}, f32[1,1,256]{2,1,0:T(1,128)}, u32[]{:S(2)}) copy-start(f32[1,1,256]{2,1,0:T(1,128)} %get-tuple-element.636) | copy-start | bytes 3076
  447.7 215.2 %copy-start.127 = (f32[1,1,256]{2,1,0:T(1,128)S(1)}, f32[1,1,256]{2,1,0:T(1,128)}, u32[]{:S(2)}) copy-start(f32[1,1,256]{2,1,0:T(1,128)} %get-tuple-element.637) | copy-start | bytes 3076
  447.7 215.3 %copy-start.73 = (f32[1,3,256]{2,1,0:T(4,128)S(1)}, f32[1,3,256]{2,1,0:T(4,128)}, u32[]{:S(2)}) copy-start(f32[1,3,256]{2,1,0:T(4,128)} %slice.1200) | copy-start | bytes 9220
  447.7 215.3 %copy-start.74 = (f32[1,3,256]{2,1,0:T(4,128)S(1)}, f32[1,3,256]{2,1,0:T(4,128)}, u32[]{:S(2)}) copy-start(f32[1,3,256]{2,1,0:T(4,128)} %slice.1231) | copy-start | bytes 9220
  447.7 215.3 %copy-start.81 = (f32[1,3,256]{2,1,0:T(4,128)S(1)}, f32[1,3,256]{2,1,0:T(4,128)}, u32[]{:S(2)}) copy-start(f32[1,3,256]{2,1,0:T(4,128)} %slice.1235) | copy-start | bytes 9220
  447.7 215.3 %copy-start.82 = (f32[1,3,256]{2,1,0:T(4,128)S(1)}, f32[1,3,256]{2,1,0:T(4,128)}, u32[]{:S(2)}) copy-start(f32[1,3,256]{2,1,0:T(4,128)} %slice.1239) | copy-start | bytes 9220
  447.7 215.4 %copy-start.122 = (f32[1,1,256]{2,1,0:T(1,128)S(1)}, f32[1,1,256]{2,1,0:T(1,128)}, u32[]{:S(2)}) copy-start(f32[1,1,256]{2,1,0:T(1,128)} %slice.1531) | copy-start | bytes 3076
  447.7 215.4 %copy-start.120 = (f32[1,1,256]{2,1,0:T(1,128)S(1)}, f32[1,1,256]{2,1,0:T(1,128)}, u32[]{:S(2)}) copy-start(f32[1,1,256]{2,1,0:T(1,128)} %slice.1508) | copy-start | bytes 3076
  447.8 215.6 %copy-start.63 = (f32[1,7,256]{2,1,0:T(8,128)S(1)}, f32[1,7,256]{2,1,0:T(8,128)}, u32[]{:S(2)}) copy-start(f32[1,7,256]{2,1,0:T(8,128)} %slice.1190) | copy-start | bytes 21508
  447.8 215.6 %copy-start.64 = (f32[1,7,256]{2,1,0:T(8,128)S(1)}, f32[1,7,256]{2,1,0:T(8,128)}, u32[]{:S(2)}) copy-start(f32[1,7,256]{2,1,0:T(8,128)} %slice.1237) | copy-start | bytes 21508
  447.8 215.6 %copy-start.77 = (f32[1,7,256]{2,1,0:T(8,128)S(1)}, f32[1,7,256]{2,1,0:T(8,128)}, u32[]{:S(2)}) copy-start(f32[1,7,256]{2,1,0:T(8,128)} %slice.1241) | copy-start | bytes 21508
  447.8 215.6 %copy-start.78 = (f32[1,7,256]{2,1,0:T(8,128)S(1)}, f32[1,7,256]{2,1,0:T(8,128)}, u32[]{:S(2)}) copy-start(f32[1,7,256]{2,1,0:T(8,128)} %slice.1245) | copy-start | bytes 21508
  493.7 169.8 %copy-start.119 = (f32[1,1,256]{2,1,0:T(1,128)S(1)}, f32[1,1,256]{2,1,0:T(1,128)}, u32[]{:S(2)}) copy-start(f32[1,1,256]{2,1,0:T(1,128)} %slice.1536) | copy-start | bytes 3076
  762.0 97.0 %copy-start.75 = (f32[1,256]{1,0:T(1,128)S(1)}, f32[1,256]{1,0:T(1,128)}, u32[]{:S(2)}) copy-start(f32[1,256]{1,0:T(1,128)} %custom-call) | copy-start | bytes 3076
  762.0 97.0 %copy-start.76 = (f32[1,256]{1,0:T(1,128)S(1)}, f32[1,256]{1,0:T(1,128)}, u32[]{:S(2)}) copy-start(f32[1,256]{1,0:T(1,128)} %custom-call.1) | copy-start | bytes 3076
  763.6 96.7 %copy-start.72 = (f32[1,256]{1,0:T(1,128)S(1)}, f32[1,256]{1,0:T(1,128)}, u32[]{:S(2)}) copy-start(f32[1,256]{1,0:T(1,128)} %get-tuple-element.346) | copy-start | bytes 3076
  874.0 223.5 %copy-start.25 = (bf16[512,256]{1,0:T(8,128)(2,1)S(1)}, bf16[512,256]{1,0:T(8,128)(2,1)}, u32[]{:S(2)}) copy-start(bf16[512,256]{1,0:T(8,128)(2,1)} %copy-done.24) | copy-start | bytes 786436
  874.0 289.1 %all-reduce.150.cloned.1.call-start = ((), (), s32[]{:S(2)}) async-start(), calls=%async_computation.1 | async-start | bytes 1048576 | tf_op jit(solution)/shard_map/psum | solution.py:135
  (104 other events, 1177.9 us)
Sparse Core Ops, SparseCore 0:
  874.1 221.3 reduce-scatter.3
  1097.8 65.2 all-reduce.149
where the time goes:
time: 1190 us; the launch traced here: 1170 us
  local copies, waits for them, and re-layouts  405 us (34%)
  blocking collectives  335 us (28%)
  waiting for transfers between devices  280 us (24%)
  other arithmetic  124 us (10%)
  between operations  17 us (1%)
    all_gather x8, blocking collectives, prefix(): everything = jax.tree.map(lambda part: lax.all_gather(part, axis), x)  335 us
    unnamed x3, waiting for transfers between devices  217 us
    slice x132, local copies, waits for them, and re-layouts, on_device(): lax.associative_scan(complex_combine, (next_re, next_im, adjoint_drive[.....  185 us
    slice x120, local copies, waits for them, and re-layouts, on_device(): lax.associative_scan(complex_combine, (lam_re, lam_im, drive_term[..., :s...  148 us
    psum x1, waiting for transfers between devices, on_device(): my_rows = lax.psum(shares, 'dp')  62.4 us
    select_n x64, other arithmetic, lap(): return jax.tree.map(lambda a, b: jnp.where(reached, a, b), new, before)  38.3 us
  transfers between devices with their start and end apart: 2, of which 2 were waited for; matrix products, arithmetic and copies ran while one was open for 1% of the time, Pallas kernels for 0%

commit v1 on v0

--- a/solution.py
+++ b/solution.py
@@ -132,7 +132,11 @@
         scatter_dimension=0,
         tiled=True,
     )
-    my_rows = lax.psum(shares, "dp")
+
+    def run_field(matrix):
+        return lax.all_gather(matrix, "dp").sum(axis=0)
+
+    my_rows = run_field(shares)
     return (outputs, input_grad, my_rows[:, : 2 * state_count], my_rows[:, 2 * state_count :])
 
 

time: 1190 us -> 1150 us (0.966)
  waiting for transfers between devices: 280 us -> 243 us
    reduce_scatter x0 -> x1, waiting for transfers between devices: none -> 221 us  [on_device(): lax.psum_scatter(jnp.concatenate([grad_in_part, grad_out_part], axis=1) *...]
    unnamed x3 -> x2, waiting for transfers between devices: 217 us -> 0.03 us
    psum x1 -> x0, waiting for transfers between devices: 62.4 us -> none  [on_device(): my_rows = lax.psum(shares, 'dp')]
    all_gather x0 -> x1, waiting for transfers between devices: none -> 21.9 us  [run_field(): return lax.all_gather(matrix, 'dp').sum(axis=0)]
  transfers between devices with their start and end apart: 2 -> 2, of which waited for: 2 -> 2; matrix products, arithmetic and copies ran while one was open for 1% -> 0% of each run, Pallas kernels for 0% -> 0%
where the time goes in v1:
time: 1150 us; the launch traced here: 1130 us
  local copies, waits for them, and re-layouts  400 us (35%)
  blocking collectives  335 us (29%)
  waiting for transfers between devices  243 us (21%)
  other arithmetic  127 us (11%)
  between operations  17.1 us (1%)
    all_gather x8, blocking collectives, prefix(): everything = jax.tree.map(lambda part: lax.all_gather(part, axis), x)  335 us
    reduce_scatter x1, waiting for transfers between devices, on_device(): lax.psum_scatter(jnp.concatenate([grad_in_part, grad_out_part], axis=1) *...  221 us
    slice x132, local copies, waits for them, and re-layouts, on_device(): lax.associative_scan(complex_combine, (next_re, next_im, adjoint_drive[.....  185 us
    slice x120, local copies, waits for them, and re-layouts, on_device(): lax.associative_scan(complex_combine, (lam_re, lam_im, drive_term[..., :s...  148 us
    select_n x64, other arithmetic, lap(): return jax.tree.map(lambda a, b: jnp.where(reached, a, b), new, before)  40.6 us
    add x28, other arithmetic, complex_combine(): later_are * early_bim + later_aim * early_bre + later_bim  23.6 us
    pad x64, local copies, waits for them, and re-layouts, on_device(): lax.associative_scan(complex_combine, (next_re, next_im, adjoint_drive[.....  23.1 us
  transfers between devices with their start and end apart: 2, of which 2 were waited for; matrix products, arithmetic and copies ran while one was open for 0% of the time, Pallas kernels for 0%

profile of v1, /device:TPU:8, one launch (start us, length us, event | category | flops | bytes accessed | tf_op | source)
XLA Modules:
  0.0 1133.1 jit_solution(5485342215908645795)
XLA Ops:
  8.0 2.7 fusion.12
  29.5 3.0 slice.1317
  32.4 3.0 slice.1323
  36.7 3.0 slice.1333
  39.7 3.0 slice.1320
  42.7 3.0 slice.1326
  45.7 3.0 slice.1328
  223.1 3.0 slice.1453
  226.1 3.0 slice.1458
  229.1 3.0 slice.1496
  442.6 4.7 rev.19
  447.4 45.9 %all_gather.38 = f32[32,1,256]{2,1,0:T(1,128)S(1)} all-gather(f32[1,1,256]{2,1,0:T(1,128)} %get-tuple-element.440), channel_id=1, replica_groups=mesh['dp'=8,'context'=32] {'context'}, dimensions={0}, use_global_device_ids=true | all-gather | bytes 33792 | tf_op jit(solution)/shard_map/all_gather | solution.py:9
  493.3 40.8 %all_gather.39 = f32[32,1,256]{2,1,0:T(1,128)S(1)} all-gather(f32[1,1,256]{2,1,0:T(1,128)} %get-tuple-element.439), channel_id=1, replica_groups=mesh['dp'=8,'context'=32] {'context'}, dimensions={0}, use_global_device_ids=true | all-gather | bytes 33792 | tf_op jit(solution)/shard_map/all_gather | solution.py:9
  534.1 41.9 %all_gather.40 = f32[32,1,256]{2,1,0:T(1,128)S(1)} all-gather(f32[1,1,256]{2,1,0:T(1,128)} %get-tuple-element.438), channel_id=1, replica_groups=mesh['dp'=8,'context'=32] {'context'}, dimensions={0}, use_global_device_ids=true | all-gather | bytes 33792 | tf_op jit(solution)/shard_map/all_gather | solution.py:9
  576.0 40.8 %all_gather.41 = f32[32,1,256]{2,1,0:T(1,128)S(1)} all-gather(f32[1,1,256]{2,1,0:T(1,128)} %get-tuple-element.437), channel_id=1, replica_groups=mesh['dp'=8,'context'=32] {'context'}, dimensions={0}, use_global_device_ids=true | all-gather | bytes 33792 | tf_op jit(solution)/shard_map/all_gather | solution.py:9
  616.8 40.0 %while.35 = (s32[]{:T(128)}, f32[1,256]{1,0:T(1,128)}, f32[1,256]{1,0:T(1,128)}, s32[]{:T(128)}, f32[32,1,256]{2,1,0:T(1,128)S(1)}, /*index=5*/f32[32,1,256]{2,1...) while((s32[]{:T(128)}, f32[1,256]{1,0:T(1,128)}, ...), condition=%wide.region_3.4_spmd.clone, body=%wide.region_2.3_spmd.clone.sunk | while | flops 3080 | bytes 8379 | solution.py:20
  656.9 2.6 rev.17
  659.5 2.6 rev.16
  662.2 2.6 rev.18
  679.3 41.9 %all_gather.37 = f32[32,1,256]{2,1,0:T(1,128)S(1)} all-gather(f32[1,1,256]{2,1,0:T(1,128)S(1)} %slice_add_fusion.64), channel_id=1, replica_groups=mesh['dp'=8,'context'=32] {'context'}, dimensions={0}, use_global_device_ids=true | all-gather | bytes 33792 | tf_op jit(solution)/shard_map/all_gather | solution.py:9
  723.3 40.7 %all_gather.35 = f32[32,1,256]{2,1,0:T(1,128)S(1)} all-gather(f32[1,1,256]{2,1,0:T(1,128)S(1)} %slice_add_fusion.66), channel_id=1, replica_groups=mesh['dp'=8,'context'=32] {'context'}, dimensions={0}, use_global_device_ids=true | all-gather | bytes 33792 | tf_op jit(solution)/shard_map/all_gather | solution.py:9
  765.7 2.7 pad.510
  768.4 2.7 pad.511
  771.8 41.9 %all_gather.34 = f32[32,1,256]{2,1,0:T(1,128)S(1)} all-gather(f32[1,1,256]{2,1,0:T(1,128)S(1)} %slice_add_fusion.67), channel_id=1, replica_groups=mesh['dp'=8,'context'=32] {'context'}, dimensions={0}, use_global_device_ids=true | all-gather | bytes 33792 | tf_op jit(solution)/shard_map/all_gather | solution.py:9
  813.7 2.6 pad.477
  817.0 2.6 pad.476
  820.3 40.7 %all_gather.36 = f32[32,1,256]{2,1,0:T(1,128)S(1)} all-gather(f32[1,1,256]{2,1,0:T(1,128)S(1)} %slice_add_fusion.65), channel_id=1, replica_groups=mesh['dp'=8,'context'=32] {'context'}, dimensions={0}, use_global_device_ids=true | all-gather | bytes 33792 | tf_op jit(solution)/shard_map/all_gather | solution.py:9
  868.0 2.6 maximum_multiply_fusion
  870.7 5.4 copy.14
  876.1 221.4 %reduce-scatter.4.cloned.1.call-done = f32[32,1024]{1,0:T(8,128)} async-done(((f32[1024,1024]{1,0:T(8,128)}), f32[32,1024]{1,0:T(8,128)}) %reduce-scatter.4.cloned.1.call-update) | async-done | bytes 131088 | tf_op jit(solution)/shard_map/reduce_scatter | solution.py:129
  1097.6 3.1 fusion.5
  1102.4 21.9 %all-gather.3.cloned.1.call-done = f32[256,1024]{1,0:T(8,128)} async-done(((f32[32,1024]{1,0:T(8,128)}), f32[256,1024]{1,0:T(8,128)}) %all-gather.3.cloned.1.call-update) | async-done | bytes 1048592 | tf_op jit(solution)/shard_map/all_gather | solution.py:137
  (910 shorter events, 475.0 us)
Async XLA Ops:
  7.2 1090.3 %reduce-scatter.4.cloned.1.call-start = ((), (), s32[]{:S(2)}) async-start(), calls=%async_computation.2 | async-start | bytes 4325376 | tf_op jit(solution)/shard_map/reduce_scatter | solution.py:129
  65.6 103.9 %copy-start.36 = (f32[1,128,256]{2,1,0:T(8,128)}, f32[1,128,256]{2,1,0:T(8,128)S(1)}, u32[]{:S(2)}) copy-start(f32[1,128,256]{2,1,0:T(8,128)S(1)} %get-tuple-element.502) | copy-start | bytes 393220
  290.4 125.1 %copy-start.19 = (f32[1,256,256]{2,1,0:T(8,128)}, f32[1,256,256]{2,1,0:T(8,128)S(1)}, u32[]{:S(2)}) copy-start(f32[1,256,256]{2,1,0:T(8,128)S(1)} %get-tuple-element.463) | copy-start | bytes 786436
  303.7 104.0 %copy-start.37 = (f32[1,128,256]{2,1,0:T(8,128)}, f32[1,128,256]{2,1,0:T(8,128)S(1)}, u32[]{:S(2)}) copy-start(f32[1,128,256]{2,1,0:T(8,128)S(1)} %get-tuple-element.510) | copy-start | bytes 393220
  423.7 235.8 %copy-start.12 = (f32[1,512,256]{2,1,0:T(8,128)S(1)}, f32[1,512,256]{2,1,0:T(8,128)}, u32[]{:S(2)}) copy-start(f32[1,512,256]{2,1,0:T(8,128)} %add.1247) | copy-start | bytes 1572868
  425.1 231.7 %copy-start.13 = (f32[1,512,256]{2,1,0:T(8,128)S(1)}, f32[1,512,256]{2,1,0:T(8,128)}, u32[]{:S(2)}) copy-start(f32[1,512,256]{2,1,0:T(8,128)} %add.1272) | copy-start | bytes 1572868
  426.5 235.7 %copy-start.14 = (f32[1,512,256]{2,1,0:T(8,128)S(1)}, f32[1,512,256]{2,1,0:T(8,128)}, u32[]{:S(2)}) copy-start(f32[1,512,256]{2,1,0:T(8,128)} %add.1274) | copy-start | bytes 1572868
  442.5 222.3 %copy-start.129 = (f32[1,1,256]{2,1,0:T(1,128)S(1)}, f32[1,1,256]{2,1,0:T(1,128)}, u32[]{:S(2)}) copy-start(f32[1,1,256]{2,1,0:T(1,128)} %get-tuple-element.599) | copy-start | bytes 3076
  442.5 222.3 %copy-start.130 = (f32[1,1,256]{2,1,0:T(1,128)S(1)}, f32[1,1,256]{2,1,0:T(1,128)}, u32[]{:S(2)}) copy-start(f32[1,1,256]{2,1,0:T(1,128)} %get-tuple-element.600) | copy-start | bytes 3076
  442.5 222.3 %copy-start.131 = (f32[1,1,256]{2,1,0:T(1,128)S(1)}, f32[1,1,256]{2,1,0:T(1,128)}, u32[]{:S(2)}) copy-start(f32[1,1,256]{2,1,0:T(1,128)} %get-tuple-element.619) | copy-start | bytes 3076
  442.5 222.3 %copy-start.132 = (f32[1,1,256]{2,1,0:T(1,128)S(1)}, f32[1,1,256]{2,1,0:T(1,128)}, u32[]{:S(2)}) copy-start(f32[1,1,256]{2,1,0:T(1,128)} %get-tuple-element.630) | copy-start | bytes 3076
  442.5 222.3 %copy-start.91 = (f32[1,2,256]{2,1,0:T(2,128)S(1)}, f32[1,2,256]{2,1,0:T(2,128)}, u32[]{:S(2)}) copy-start(f32[1,2,256]{2,1,0:T(2,128)} %get-tuple-element.640) | copy-start | bytes 6148
  442.6 222.3 %copy-start.90 = (f32[1,2,256]{2,1,0:T(2,128)S(1)}, f32[1,2,256]{2,1,0:T(2,128)}, u32[]{:S(2)}) copy-start(f32[1,2,256]{2,1,0:T(2,128)} %get-tuple-element.639) | copy-start | bytes 6148
  447.3 217.6 %copy-start.127 = (f32[1,1,256]{2,1,0:T(1,128)S(1)}, f32[1,1,256]{2,1,0:T(1,128)}, u32[]{:S(2)}) copy-start(f32[1,1,256]{2,1,0:T(1,128)} %get-tuple-element.628) | copy-start | bytes 3076
  447.3 217.6 %copy-start.128 = (f32[1,1,256]{2,1,0:T(1,128)S(1)}, f32[1,1,256]{2,1,0:T(1,128)}, u32[]{:S(2)}) copy-start(f32[1,1,256]{2,1,0:T(1,128)} %get-tuple-element.629) | copy-start | bytes 3076
  447.3 217.7 %copy-start.74 = (f32[1,3,256]{2,1,0:T(4,128)S(1)}, f32[1,3,256]{2,1,0:T(4,128)}, u32[]{:S(2)}) copy-start(f32[1,3,256]{2,1,0:T(4,128)} %slice.1200) | copy-start | bytes 9220
  447.3 217.7 %copy-start.75 = (f32[1,3,256]{2,1,0:T(4,128)S(1)}, f32[1,3,256]{2,1,0:T(4,128)}, u32[]{:S(2)}) copy-start(f32[1,3,256]{2,1,0:T(4,128)} %slice.1231) | copy-start | bytes 9220
  447.3 217.8 %copy-start.82 = (f32[1,3,256]{2,1,0:T(4,128)S(1)}, f32[1,3,256]{2,1,0:T(4,128)}, u32[]{:S(2)}) copy-start(f32[1,3,256]{2,1,0:T(4,128)} %slice.1235) | copy-start | bytes 9220
  447.3 217.8 %copy-start.83 = (f32[1,3,256]{2,1,0:T(4,128)S(1)}, f32[1,3,256]{2,1,0:T(4,128)}, u32[]{:S(2)}) copy-start(f32[1,3,256]{2,1,0:T(4,128)} %slice.1239) | copy-start | bytes 9220
  447.3 217.8 %copy-start.123 = (f32[1,1,256]{2,1,0:T(1,128)S(1)}, f32[1,1,256]{2,1,0:T(1,128)}, u32[]{:S(2)}) copy-start(f32[1,1,256]{2,1,0:T(1,128)} %slice.1531) | copy-start | bytes 3076
  447.3 217.8 %copy-start.121 = (f32[1,1,256]{2,1,0:T(1,128)S(1)}, f32[1,1,256]{2,1,0:T(1,128)}, u32[]{:S(2)}) copy-start(f32[1,1,256]{2,1,0:T(1,128)} %slice.1508) | copy-start | bytes 3076
  447.3 218.0 %copy-start.64 = (f32[1,7,256]{2,1,0:T(8,128)S(1)}, f32[1,7,256]{2,1,0:T(8,128)}, u32[]{:S(2)}) copy-start(f32[1,7,256]{2,1,0:T(8,128)} %slice.1190) | copy-start | bytes 21508
  447.4 218.0 %copy-start.65 = (f32[1,7,256]{2,1,0:T(8,128)S(1)}, f32[1,7,256]{2,1,0:T(8,128)}, u32[]{:S(2)}) copy-start(f32[1,7,256]{2,1,0:T(8,128)} %slice.1237) | copy-start | bytes 21508
  447.4 218.0 %copy-start.78 = (f32[1,7,256]{2,1,0:T(8,128)S(1)}, f32[1,7,256]{2,1,0:T(8,128)}, u32[]{:S(2)}) copy-start(f32[1,7,256]{2,1,0:T(8,128)} %slice.1241) | copy-start | bytes 21508
  447.4 218.0 %copy-start.79 = (f32[1,7,256]{2,1,0:T(8,128)S(1)}, f32[1,7,256]{2,1,0:T(8,128)}, u32[]{:S(2)}) copy-start(f32[1,7,256]{2,1,0:T(8,128)} %slice.1245) | copy-start | bytes 21508
  493.3 172.2 %copy-start.120 = (f32[1,1,256]{2,1,0:T(1,128)S(1)}, f32[1,1,256]{2,1,0:T(1,128)}, u32[]{:S(2)}) copy-start(f32[1,1,256]{2,1,0:T(1,128)} %slice.1536) | copy-start | bytes 3076
  764.0 97.0 %copy-start.76 = (f32[1,256]{1,0:T(1,128)S(1)}, f32[1,256]{1,0:T(1,128)}, u32[]{:S(2)}) copy-start(f32[1,256]{1,0:T(1,128)} %custom-call) | copy-start | bytes 3076
  764.0 97.0 %copy-start.77 = (f32[1,256]{1,0:T(1,128)S(1)}, f32[1,256]{1,0:T(1,128)}, u32[]{:S(2)}) copy-start(f32[1,256]{1,0:T(1,128)} %custom-call.1) | copy-start | bytes 3076
  765.7 96.7 %copy-start.73 = (f32[1,256]{1,0:T(1,128)S(1)}, f32[1,256]{1,0:T(1,128)}, u32[]{:S(2)}) copy-start(f32[1,256]{1,0:T(1,128)} %get-tuple-element.346) | copy-start | bytes 3076
  876.0 221.5 %copy-start.25 = (bf16[512,256]{1,0:T(8,128)(2,1)S(1)}, bf16[512,256]{1,0:T(8,128)(2,1)}, u32[]{:S(2)}) copy-start(bf16[512,256]{1,0:T(8,128)(2,1)} %copy-done.24) | copy-start | bytes 786436
  876.0 221.5 %copy-start.135 = (f32[1024]{0:T(1024)S(1)}, f32[1024]{0:T(1024)}, u32[]{:S(2)}) copy-start(f32[1024]{0:T(1024)} %param.18) | copy-start | bytes 12292
  876.1 248.2 %all-gather.3.cloned.1.call-start = ((), (), s32[]{:S(2)}) async-start(), calls=%async_computation.1 | async-start | bytes 1179648 | tf_op jit(solution)/shard_map/all_gather | solution.py:137
  (106 other events, 1196.9 us)
Sparse Core Ops, SparseCore 0:
  876.2 221.2 reduce-scatter.3
  1099.4 24.8 all-gather.2
